TPU v7x, 32 devices: a whole 2x2x4 slice. The times are simulated.
32 devices in a mesh: ctx: 8 (over y, x, core), mp: 4 (over z).
Axes of the slice: x: 2, y: 2, z: 4, core: 2. Of those that a mesh axis runs over, the one named last changes fastest.
Arguments:
- resid_in: bfloat16 [4096, 8192], P('ctx', 'mp'), may hold values from -6 to 6
- q_mr: bfloat16 [4096, 8192], P('ctx', 'mp'), may hold values from -6 to 6
- k_mr: bfloat16 [4096, 8192], P('ctx', 'mp'), may hold values from -6 to 6
- v_mr: bfloat16 [4096, 8192], P('ctx', 'mp'), may hold values from -6 to 6
- mr_filter: float32 [128, 8192], P(None, 'mp'), may hold values from -0.5 to 0.5
- mr_out: bfloat16 [8192, 8192], P('ctx', 'mp'), may hold values from -0.0625 to 0.0625
- q_li: bfloat16 [4096, 8192], P('ctx', 'mp'), may hold values from -6 to 6
- k_li: bfloat16 [4096, 8192], P('ctx', 'mp'), may hold values from -6 to 6
- li_rate: float32 [8192], P('mp'), may hold values from 2.4414063e-05 to 0.0333333333
- li_residue: float32 [8192], P('mp'), may hold values from 0.5 to 2
Outputs:
- mixed: bfloat16 [4096, 8192], P('ctx', 'mp')
- long_out: bfloat16 [4096, 8192], P('ctx', 'mp')
All inputs are finite; a program needn't handle non-finite values.
Results may differ from a plain program's by a relative error of at most 0.008.
Values may be sent and summed in bfloat16 or wider, within the bound.
A program may use at most 192 MiB of HBM per device.

v0:
```python
import jax
import jax.numpy as jnp
from jax import lax
from jax.sharding import PartitionSpec as P


def passed_along(value, axis, by):
    peers = lax.axis_size(axis)
    pairs = [(i, i + by) for i in range(peers) if 0 <= i + by < peers]
    return lax.ppermute(value, axis, pairs)


def carried_in(value, axis, join, neutral):
    count, mine = (lax.axis_size(axis), lax.axis_index(axis))
    pieces = jax.tree.map(lambda part: lax.all_gather(part, axis), value)
    subtotal = jax.tree.map(
        lambda part, zero: jnp.full_like(part, 0) + jnp.asarray(zero, part.dtype), value, neutral
    )

    def step(position, subtotal):
        longer = join(subtotal, jax.tree.map(lambda part: part[position], pieces))
        return jax.tree.map(lambda new, old: jnp.where(position < mine, new, old), longer, subtotal)

    return lax.fori_loop(0, count - 1, step, subtotal)


def link_pair(earlier, later):
    return (earlier[0] * later[0], later[0] * earlier[1] + later[1])


def body(resid_in, q_mr, k_mr, v_mr, mr_filter, mr_out, q_li, k_li, li_rate, li_residue):
    row_count = q_mr.shape[0]
    chan_count = q_mr.shape[1]
    tap_count = mr_filter.shape[0]
    drive_mr = (k_mr.astype(jnp.float32) * v_mr.astype(jnp.float32)).astype(jnp.bfloat16)
    prev_rows = passed_along(drive_mr[row_count - (tap_count - 1) :], "ctx", 1)
    padded = jnp.concatenate([prev_rows, drive_mr], 0).astype(jnp.float32)[None]
    kernel = mr_filter[::-1][:, None, :]
    filtered = lax.conv_general_dilated(
        padded,
        kernel,
        (1,),
        "VALID",
        dimension_numbers=("NWC", "WIO", "NWC"),
        feature_group_count=chan_count,
        precision=lax.Precision.HIGHEST,
    )[0]
    gated = (q_mr.astype(jnp.float32) * filtered).astype(jnp.bfloat16)
    gathered = lax.all_gather(gated, "mp", axis=1, tiled=True)
    all_rows = lax.all_gather(mr_out, "ctx", axis=0, tiled=True)
    summed = jnp.dot(gathered, all_rows, preferred_element_type=jnp.float32)
    mixed = (resid_in.astype(jnp.float32) + summed).astype(jnp.bfloat16)
    decay = jnp.exp(-li_rate)
    drive_li = k_li.astype(jnp.float32) * mixed.astype(jnp.float32)
    decay_rows = jnp.broadcast_to(decay[None, :], drive_li.shape)
    _, local_state = lax.associative_scan(link_pair, (decay_rows, drive_li), axis=0)
    offsets = jnp.arange(1, row_count + 1, dtype=jnp.float32)[:, None]
    powers = jnp.exp(-li_rate[None, :] * offsets)
    block_end = local_state[row_count - 1]
    block_decay = jnp.exp(-li_rate * row_count)
    identity = (jnp.ones_like(block_decay), jnp.zeros_like(block_end))
    prefix = carried_in((block_decay, block_end), "ctx", link_pair, identity)
    carried = prefix[1]
    state = local_state + powers * carried[None, :]
    scale = li_residue * jnp.sqrt(-jnp.expm1(-2.0 * li_rate))
    long_out = (q_li.astype(jnp.float32) * scale * state).astype(jnp.bfloat16)
    return (mixed, long_out)


def solution(mesh):
    in_specs = (
        P("ctx", "mp"),
        P("ctx", "mp"),
        P("ctx", "mp"),
        P("ctx", "mp"),
        P(None, "mp"),
        P("ctx", "mp"),
        P("ctx", "mp"),
        P("ctx", "mp"),
        P("mp"),
        P("mp"),
    )
    out_specs = (P("ctx", "mp"), P("ctx", "mp"))
    return jax.shard_map(body, mesh=mesh, in_specs=in_specs, out_specs=out_specs, check_vma=False)
```

profile of v0, /device:TPU:0, one launch (start us, length us, event | category | flops | bytes accessed | tf_op | source)
XLA Modules:
  0.0 563.9 jit_solution(2799196935869276048)
XLA Ops:
  7.2 3.1 multiply_convert_fusion.1
  10.3 0.9 slice.256
  11.2 3.2 collective-permute-start
  14.4 5.2 rev.3
  19.6 1.8 maximum_bitcast_fusion
  21.4 45.6 %fusion = f32[1,512,2048]{2,0,1:T(1,128)S(1)} fusion(bf16[1,639,2048]{2,1,0:T(8,128)(2,1)S(1)} %maximum_bitcast_fusion, f32[128,1,2048]{2,0,1:T(8,128)S(1)} %bitcast.22), kind=kOutput, calls=%fused_computation.3 | convolution fusion | flops 1610612736 | bytes 7860224 | tf_op jit(solution)/shard_map/conv_general_dilated | solution.py:39
  67.0 2.9 fusion.2
  70.0 0.7 all-gather.7.cloned.1.call-update
  71.4 14.1 %all-gather = f32[16384]{0:T(1024)S(1)} all-gather(f32[2048]{0:T(1024)S(1)} %get-tuple-element.139), channel_id=2, replica_groups=mesh['ctx'=8,'mp'=4] {'ctx'}, dimensions={0}, use_global_device_ids=true | all-gather | bytes 73728 | tf_op jit(solution)/shard_map/all_gather | solution.py:15
  86.8 138.0 %all-gather.5.cloned.1.call-done = bf16[512,8192]{1,0:T(8,128)(2,1)} async-done(((bf16[512,2048]{1,0:T(8,128)(2,1)}), bf16[512,8192]{1,0:T(8,128)(2,1)}) %all-gather.5.cloned.1.call-update) | async-done | bytes 8388624 | tf_op jit(solution)/shard_map/all_gather | solution.py:49
  224.8 160.9 %all-gather.7.cloned.1.call-done = bf16[8192,2048]{1,0:T(8,128)(2,1)} async-done(((bf16[1024,2048]{1,0:T(8,128)(2,1)}), bf16[8192,2048]{1,0:T(8,128)(2,1)}) %all-gather.7.cloned.1.call-update) | async-done | bytes 33554448 | tf_op jit(solution)/shard_map/all_gather | solution.py:50
  385.6 25.6 %convert_multiply_fusion = (f32[512,2048]{1,0:T(8,128)}, bf16[512,2048]{1,0:T(8,128)(2,1)}) fusion(bf16[512,2048]{1,0:T(8,128)(2,1)} %param.19, bf16[512,8192]{1,0:T(8,128)(2,1)} %all-gather.5.cloned.1.call-done, bf16[8192,2048]{1,0:T(8,128)(2,1)} %all-gather.7.cloned.1.call-done, bf16[512,2048]{1,0:T(8,128)(2,1)} %param.12), kind=kOutput, calls=%fused_computation.8 | convolution fusion | flops 17186160640 | bytes 52428800 | tf_op jit(solution)/shard_map/dot_general | solution.py:51
  411.3 10.0 %slice.254 = f32[255,2048]{1,0:T(8,128)} slice(f32[512,2048]{1,0:T(8,128)} %get-tuple-element.143), slice={[2:512:2], [0:2048:1]} | slice | bytes 4177920 | tf_op jit(solution)/shard_map/slice | solution.py:56
  421.3 9.8 %slice.200 = f32[256,2048]{1,0:T(8,128)} slice(f32[512,2048]{1,0:T(8,128)} %get-tuple-element.143), slice={[1:512:2], [0:2048:1]} | slice | bytes 4194304 | tf_op jit(solution)/shard_map/slice | solution.py:56
  431.1 9.8 %slice.199 = f32[256,2048]{1,0:T(8,128)} slice(f32[512,2048]{1,0:T(8,128)} %get-tuple-element.143), slice={[0:511:2], [0:2048:1]} | slice | bytes 4194304 | tf_op jit(solution)/shard_map/slice | solution.py:56
  440.9 2.6 multiply_add_fusion
  443.5 2.9 slice.205
  446.4 2.8 slice.204
  449.3 1.7 multiply_add_fusion.1
  450.9 1.7 slice.250
  452.7 1.5 slice.210
  454.1 1.5 slice.209
  455.6 2.1 multiply_add_fusion.2
  457.7 1.7 slice.215
  459.4 1.7 slice.214
  461.1 1.1 multiply_add_fusion.3
  462.1 0.7 slice.246
  462.8 0.7 slice.220
  464.2 1.0 multiply_add_fusion.4
  466.5 1.5 multiply_add_fusion.5
  468.0 1.5 slice.242
  469.5 1.5 slice.230
  471.0 1.4 slice.229
  472.4 1.4 multiply_add_fusion.6
  473.8 1.4 slice.235
  475.2 1.4 slice.234
  478.4 1.1 slice.248
  479.6 3.0 slice.252
  482.6 1.4 slice.257
  484.0 0.7 multiply_add_fusion.7
  484.7 0.7 slice_add_fusion.1
  485.5 0.9 fusion.16
  486.5 0.8 fusion.10
  489.3 0.9 copy-done.2
  490.2 1.1 add.181
  491.3 4.2 pad.70
  495.6 1.8 fusion.4
  497.4 4.9 pad.69
  502.3 3.4 add.183
  505.7 0.7 fusion.3
  506.4 1.5 pad_maximum_fusion
  507.9 16.7 %pad.71 = f32[512,2048]{1,0:T(8,128)} pad(f32[256,2048]{1,0:T(8,128)} %pad_maximum_fusion, f32[]{:T(128)} %constant.35.clone.1), padding=0_1_1x0_0_0 | pad | bytes 6291460 | tf_op jit(solution)/shard_map/pad | solution.py:56
  524.7 9.1 %pad.72 = f32[512,2048]{1,0:T(8,128)} pad(f32[256,2048]{1,0:T(8,128)S(1)} %copy-done.3, f32[]{:T(128)} %constant.35.clone.1), padding=1_0_1x0_0_0 | pad | bytes 6291460 | tf_op jit(solution)/shard_map/pad | solution.py:56
  533.7 0.9 add_bitcast_fusion
  534.6 9.2 %all-gather.1 = f32[8,1,2048]{2,1,0:T(1,128)S(1)} all-gather(f32[1,1,2048]{2,1,0:T(1,128)S(1)} %add_bitcast_fusion), channel_id=1, replica_groups=mesh['ctx'=8,'mp'=4] {'ctx'}, dimensions={0}, use_global_device_ids=true | all-gather | bytes 73728 | tf_op jit(solution)/shard_map/all_gather | solution.py:15
  543.8 6.3 %while.14 = (s32[]{:T(128)}, f32[2048]{0:T(1024)S(1)}, s32[]{:T(128)}, f32[8,2048]{1,0:T(8,128)}, f32[8,2048]{1,0:T(8,128)S(1)}, /*index=5*/s32[]{:T(128)}, s32[]{:T(128)}) while((s32[]{:T(128)}, f32[2048]{0:T(1024)S(1)}, s32[]{:T(128)}, f32[8,2048]{1,0:T(8,128)}, f32[8,2048]{1,0:T(8,128)S(1)}, /*index=5*/s32[]{:T(128)}, ...), condition=%wide.region_1.2_spmd.clone, body=%wide.region_0.1_spmd.clone.sunk | while | flops 8196 | bytes 65645 | solution.py:24
  543.8 0.9 constant_dynamic-slice_fusion.3
  544.7 0.9 constant_dynamic-slice_fusion.3
  545.6 0.9 constant_dynamic-slice_fusion.3
  546.5 0.9 constant_dynamic-slice_fusion.3
  547.4 0.9 constant_dynamic-slice_fusion.3
  548.3 0.9 constant_dynamic-slice_fusion.3
  549.2 0.9 constant_dynamic-slice_fusion.3
  550.2 6.9 %multiply_convert_fusion = bf16[512,2048]{1,0:T(8,128)(2,1)} fusion(f32[512,2048]{1,0:T(8,128)} %pad.71, f32[512,2048]{1,0:T(8,128)} %pad.72, bf16[512,2048]{1,0:T(8,128)(2,1)} %param.18, f32[2048]{0:T(1024)S(1)} %get-tuple-element.96, f32[512]{0:T(512)S(1)} %copy-done.28, f32[2048]{0:T(1024)S(1)} %copy-done.24, f32[2048]{0:T(1024)S(1)} %copy-done.23), kind=kLoop, calls=%fused_computation.7 | loop fusion | flops 8388608 | bytes 12609536 | tf_op jit(solution)/shard_map/convert_element_type | solution.py:66
  (120 shorter events, 7.9 us)
Async XLA Ops:
  7.2 7.2 %copy-start.8 = (f32[128,2048]{1,0:T(8,128)S(1)}, f32[128,2048]{1,0:T(8,128)}, u32[]{:S(2)}) copy-start(f32[128,2048]{1,0:T(8,128)} %param.16) | copy-start | bytes 3145732
  7.2 217.6 %all-gather.5.cloned.1.call-start = ((), (), s32[]{:S(2)}) async-start(), calls=%async_computation | async-start | bytes 10485760 | tf_op jit(solution)/shard_map/all_gather | solution.py:49
  11.2 8.3 %collective-permute-start = (bf16[127,2048]{1,0:T(8,128)(2,1)}, bf16[127,2048]{1,0:T(8,128)(2,1)}, u32[]{:S(2)}, u32[]{:S(2)}) collective-permute-start(bf16[127,2048]{1,0:T(8,128)(2,1)} %slice.256), channel_id=1, source_target_pairs={{0,4},{4,8},{8,12},{12,16},{16,20},{20,24},{24,28},{1,5},{5,9},{9,... | collective-permute-start | bytes 1560584 | tf_op jit(solution)/shard_map/ppermute | solution.py:10
  19.6 1.8 copy-start.9
  21.4 45.6 %copy-start.7 = (bf16[512,2048]{1,0:T(8,128)(2,1)S(1)}, bf16[512,2048]{1,0:T(8,128)(2,1)}, u32[]{:S(2)}) copy-start(bf16[512,2048]{1,0:T(8,128)(2,1)} %param.13) | copy-start | bytes 6291460
  69.9 0.8 copy-start.29
  69.9 0.8 copy-start.30
  69.9 315.7 %all-gather.7.cloned.1.call-start = ((), (), s32[]{:S(2)}) async-start(), calls=%async_computation.1 | async-start | bytes 37748736 | tf_op jit(solution)/shard_map/all_gather | solution.py:50
  71.3 369.6 %copy-start.12 = (f32[2048]{0:T(1024)}, f32[2048]{0:T(1024)S(1)}, u32[]{:S(2)}) copy-start(f32[2048]{0:T(1024)S(1)} %get-tuple-element.138) | copy-start | bytes 24580
  71.3 377.9 %copy-start.14 = (f32[2048]{0:T(1024)}, f32[2048]{0:T(1024)S(1)}, u32[]{:S(2)}) copy-start(f32[2048]{0:T(1024)S(1)} %get-tuple-element.141) | copy-start | bytes 24580
  71.3 384.2 %copy-start.16 = (f32[2048]{0:T(1024)}, f32[2048]{0:T(1024)S(1)}, u32[]{:S(2)}) copy-start(f32[2048]{0:T(1024)S(1)} %get-tuple-element.140) | copy-start | bytes 24580
  71.3 389.7 %copy-start.18 = (f32[2048]{0:T(1024)}, f32[2048]{0:T(1024)S(1)}, u32[]{:S(2)}) copy-start(f32[2048]{0:T(1024)S(1)} %get-tuple-element.132) | copy-start | bytes 24580
  71.4 392.9 %copy-start.20 = (f32[2048]{0:T(1024)}, f32[2048]{0:T(1024)S(1)}, u32[]{:S(2)}) copy-start(f32[2048]{0:T(1024)S(1)} %get-tuple-element.133) | copy-start | bytes 24580
  443.5 39.1 %copy-start.1 = (f32[256,2048]{1,0:T(8,128)}, f32[256,2048]{1,0:T(8,128)S(1)}, u32[]{:S(2)}) copy-start(f32[256,2048]{1,0:T(8,128)S(1)} %multiply_add_fusion) | copy-start | bytes 6291460
  450.9 28.6 %copy-start.5 = (f32[128,2048]{1,0:T(8,128)}, f32[128,2048]{1,0:T(8,128)S(1)}, u32[]{:S(2)}) copy-start(f32[128,2048]{1,0:T(8,128)S(1)} %multiply_add_fusion.1) | copy-start | bytes 3145732
  468.0 19.3 %slice-start.3 = ((f32[8,2048]{1,0:T(8,128)}), f32[1,2048]{1,0:T(1,128)S(1)}, s32[]{:S(2)}) async-start(f32[8,2048]{1,0:T(8,128)} %multiply_add_fusion.5), calls=%async_computation.5 | async-start | bytes 16384 | tf_op jit(solution)/shard_map/slice | solution.py:56
  477.8 9.8 %copy-start.10 = (f32[15,2048]{1,0:T(8,128)S(1)}, f32[15,2048]{1,0:T(8,128)}, u32[]{:S(2)}) copy-start(f32[15,2048]{1,0:T(8,128)} %slice.246) | copy-start | bytes 368644
  479.5 7.9 %copy-start.11 = (f32[7,2048]{1,0:T(8,128)S(1)}, f32[7,2048]{1,0:T(8,128)}, u32[]{:S(2)}) copy-start(f32[7,2048]{1,0:T(8,128)} %slice.244) | copy-start | bytes 172036
  479.6 7.9 %copy-start.22 = (f32[2048]{0:T(1024)S(1)}, f32[2048]{0:T(1024)}, u32[]{:S(2)}) copy-start(f32[2048]{0:T(1024)} %get-tuple-element.135) | copy-start | bytes 24580
  479.6 7.9 %copy-start.27 = (f32[1,2048]{1,0:T(1,128)S(1)}, f32[1,2048]{1,0:T(1,128)}, u32[]{:S(2)}) copy-start(f32[1,2048]{1,0:T(1,128)} %slice.262) | copy-start | bytes 24580
  479.6 8.0 %copy-start.21 = (f32[2048]{0:T(1024)S(1)}, f32[2048]{0:T(1024)}, u32[]{:S(2)}) copy-start(f32[2048]{0:T(1024)} %copy-done.20) | copy-start | bytes 24580
  479.6 8.0 %copy-start.26 = (f32[1,2048]{1,0:T(1,128)S(1)}, f32[1,2048]{1,0:T(1,128)}, u32[]{:S(2)}) copy-start(f32[1,2048]{1,0:T(1,128)} %slice.261) | copy-start | bytes 24580
  485.5 2.4 copy-start.19
  487.4 0.7 slice-start.2
  487.7 1.0 copy-start.6
  487.8 1.0 copy-start.17
  488.1 0.7 slice-start.1
  489.2 1.0 copy-start.2
  490.2 5.3 copy-start.15
  495.5 1.8 slice-start
  502.3 3.4 copy-start
  502.3 3.4 copy-start.4
  502.3 3.4 copy-start.13
  505.7 0.7 copy-start.25
  507.9 16.7 %copy-start.3 = (f32[256,2048]{1,0:T(8,128)S(1)}, f32[256,2048]{1,0:T(8,128)}, u32[]{:S(2)}) copy-start(f32[256,2048]{1,0:T(8,128)} %add.183) | copy-start | bytes 6291460
  524.6 25.5 %copy-start.23 = (f32[2048]{0:T(1024)S(1)}, f32[2048]{0:T(1024)}, u32[]{:S(2)}) copy-start(f32[2048]{0:T(1024)} %get-tuple-element.131) | copy-start | bytes 24580
  524.7 25.5 %copy-start.24 = (f32[2048]{0:T(1024)S(1)}, f32[2048]{0:T(1024)}, u32[]{:S(2)}) copy-start(f32[2048]{0:T(1024)} %get-tuple-element.142) | copy-start | bytes 24580
  524.7 25.5 %copy-start.28 = (f32[512]{0:T(512)S(1)}, f32[512]{0:T(512)}, u32[]{:S(2)}) copy-start(f32[512]{0:T(512)} %iota_add_fusion) | copy-start | bytes 6148
Sparse Core Ops, SparseCore 0:
  70.0 154.7 all-gather.4
  226.6 158.9 all-gather.6
where the time goes:
time: 566 us; the launch traced here: 564 us
  waiting for transfers between devices  300 us (53%)
  local copies, waits for them, and re-layouts  111 us (20%)
  matrix products  71.2 us (13%)
  other arithmetic  40.3 us (7%)
  blocking collectives  23.3 us (4%)
  between operations  14.7 us (3%)
    all_gather x1, waiting for transfers between devices, body(): all_rows = lax.all_gather(mr_out, 'ctx', axis=0, tiled=True)  161 us
    all_gather x1, waiting for transfers between devices, body(): gathered = lax.all_gather(gated, 'mp', axis=1, tiled=True)  138 us
    slice x34, local copies, waits for them, and re-layouts, body(): lax.associative_scan(link_pair, (decay_rows, drive_li), axis=0)  61.5 us
    conv_general_dilated x1, matrix products, body(): lax.conv_general_dilated(padded, kernel, (1,), 'VALID', dimension_numbers...  45.6 us
    pad x16, local copies, waits for them, and re-layouts, body(): lax.associative_scan(link_pair, (decay_rows, drive_li), axis=0)  35.5 us
    dot_general x1, matrix products, body(): summed = jnp.dot(gathered, all_rows, preferred_element_type=jnp.float32)  25.6 us
    all_gather x2, blocking collectives, carried_in(): pieces = jax.tree.map(lambda part: lax.all_gather(part, axis), value)  23.3 us
    add x16, other arithmetic, link_pair(): return (earlier[0] * later[0], later[0] * earlier[1] + later[1])  16.2 us
  transfers between devices with their start and end apart: 3, of which 2 were waited for; matrix products, arithmetic and copies ran while one was open for 1% of the time, Pallas kernels for 0%

commit v1 on v0

v1 whole, which is shorter than its diff:
```python
import functools

import jax
import jax.numpy as jnp
import numpy as np
from jax import lax
from jax.experimental import pallas as pl
from jax.experimental.pallas import tpu as pltpu
from jax.sharding import PartitionSpec as P

F32 = jnp.float32
BF16 = jnp.bfloat16
PIECE = 256
LANES = 512
BLOCK = 128
MESH = pl.DeviceIdType.MESH


def split(matrix):
    high = matrix.astype(BF16)
    low = (matrix - high.astype(np.float64)).astype(BF16)
    return np.concatenate([high, low], 0)


def transforms():
    size, half = 2 * BLOCK, BLOCK
    k = np.arange(half)[:, None]
    n = np.arange(size)[None, :]
    cos = np.cos(2 * np.pi * ((k * n) % size) / size)
    sin = -np.sin(2 * np.pi * ((k * n) % size) / size)
    nyquist = np.where(np.arange(size) % 2 == 0, 1.0, -1.0)
    forward_sin = sin.copy()
    forward_sin[0] = nyquist
    forward = np.concatenate([cos, forward_sin], 0)
    cos_nyquist = cos.copy()
    cos_nyquist[0] = nyquist
    of_filter = np.concatenate([cos, sin, cos_nyquist], 0)[:, :half]
    weight = np.where(k == 0, 1.0, 2.0) / size
    back_sin = sin * weight
    back_sin[0] = nyquist / size
    back = np.concatenate([cos * weight, back_sin], 0).T[half:]
    return split(forward), split(of_filter), split(back)


def mm(a, b):
    return jnp.dot(a, b, preferred_element_type=F32)


def mm2(stacked, b):
    rows = stacked.shape[0] // 2
    both = mm(stacked, b)
    return both[:rows] + both[rows:]


def w_plan(n, pieces):
    if n == 8 and pieces % 2 == 0:
        half = pieces // 2
        first, last = list(range(half)), list(range(half, pieces))
        own = []
        for a, b in zip(first + last, last + first):
            own += [(0, a, 2), (0, b, 4), (0, a, 1)]
        events = []
        for a, b in zip(first, last):
            events.append((2, a, [4, 1]))
            events.append((4, b, [2, 1]))
        for a, b in zip(last, first):
            events.append((2, a, [1]))
            events.append((4, b, [1]))
        for a, b in zip(first, last):
            events.append((6, a, [1]))
            events.append((6, b, [1]))
        tail = [(d, p) for d in (1, 3, 5, 7) for p in range(pieces)]
        return own, events, tail
    own = [(0, p, d) for d in range(1, n) for p in range(pieces)]
    return own, [], [(d, p) for d in range(1, n) for p in range(pieces)]


def kernel(
    n, m, pieces,
    resid_hbm, q_hbm, k_hbm, v_hbm, filt_hbm, w_hbm, qli_hbm, kli_hbm, rate_ref, scale_ref,
    fwd_ref, fil_ref, back_ref,
    mixed_hbm, long_hbm,
    kbuf, vbuf, qbuf, fbuf, halo, wbuf, gbuf, acc, ends, carry,
    lsem, wsend, wrecv, gsend, grecv, hsem, esend, erecv,
):
    rows, chans = kbuf.shape
    q_count = chans // LANES
    blocks = rows // BLOCK
    me = lax.axis_index("ctx")
    z = lax.axis_index("mp")

    def local(i, src, dst):
        return pltpu.make_async_copy(src, dst, lsem.at[i])

    load_k = local(0, k_hbm, kbuf)
    load_v = local(1, v_hbm, vbuf)
    load_q = local(2, q_hbm, qbuf)
    load_f = local(3, filt_hbm, fbuf)
    own_rows = pl.ds(pl.multiple_of(me * (pieces * PIECE), PIECE), pieces * PIECE)
    load_w = local(4, w_hbm, wbuf.at[own_rows])
    for copy in (load_k, load_v, load_f, load_q, load_w):
        copy.start()

    barrier = pltpu.get_barrier_semaphore()
    for d in range(1, n):
        pl.semaphore_signal(barrier, inc=1, device_id={"ctx": lax.rem(me + d, n)}, device_id_type=MESH)

    for d in range(1, m):
        pl.semaphore_signal(barrier, inc=1, device_id={"mp": lax.rem(z + d, m)}, device_id_type=MESH)
    pl.semaphore_wait(barrier, n + m - 2)

    def peer(d):
        return me + d - 2 * d_and(d) if n & (n - 1) == 0 else None

    def d_and(d):
        total = 0
        bit = 1
        while bit < n:
            if d & bit:
                total = total + bit * lax.rem(me // bit, 2)
            bit *= 2
        return total

    def piece_rows(d, p):
        return pl.ds(pl.multiple_of((peer(d) * pieces + p) * PIECE, PIECE), PIECE)

    sends = []

    def send_w(d, p, hop):
        src = w_hbm.at[pl.ds(p * PIECE, PIECE)] if d == 0 else wbuf.at[piece_rows(d, p)]
        copy = pltpu.make_async_remote_copy(
            src_ref=src,
            dst_ref=wbuf.at[piece_rows(d, p)],
            send_sem=wsend.at[len(sends)],
            recv_sem=wrecv.at[(d ^ hop) * pieces + p],
            device_id={"ctx": peer(hop)},
            device_id_type=MESH,
        )
        copy.start()
        sends.append(copy)

    def wait_w(d, p):
        pltpu.make_async_copy(
            wbuf.at[piece_rows(d, p)], wbuf.at[piece_rows(d, p)], wrecv.at[d * pieces + p]
        ).wait()

    own, events, tail = w_plan(n, pieces)
    for d, p, hop in own:
        send_w(d, p, hop)

    load_k.wait()
    load_v.wait()

    def drive_block(b, _):
        r = pl.ds(pl.multiple_of(b * BLOCK, BLOCK), BLOCK)
        kbuf[r] = (kbuf[r].astype(F32) * vbuf[r].astype(F32)).astype(BF16)
        return 0

    drive_block(blocks - 1, 0)
    halo_copy = pltpu.make_async_remote_copy(
        src_ref=kbuf.at[pl.ds(rows - BLOCK, BLOCK)],
        dst_ref=halo,
        send_sem=hsem.at[0],
        recv_sem=hsem.at[1],
        device_id={"ctx": lax.rem(me + 1, n)},
        device_id_type=MESH,
    )
    halo_copy.start()
    lax.fori_loop(0, blocks - 1, drive_block, 0)
    load_r = local(5, resid_hbm, vbuf)
    load_r.start()
    load_f.wait()
    load_q.wait()
    halo_copy.wait_recv()

    @pl.when(me == 0)
    def _():
        halo[...] = jnp.zeros_like(halo)

    def g_copy(up, k, j):
        source = z - k if up else z + k
        slot = source * q_count + j
        sem = ((0 if up else 1) * (m - 1) + k) * q_count + j
        return pltpu.make_async_remote_copy(
            src_ref=gbuf.at[slot],
            dst_ref=gbuf.at[slot],
            send_sem=gsend.at[sem],
            recv_sem=grecv.at[sem],
            device_id={"mp": z + 1 if up else z - 1},
            device_id_type=MESH,
        )

    def g_recv(up, k, j):
        source = z - 1 - k if up else z + 1 + k
        slot = source * q_count + j
        sem = ((0 if up else 1) * (m - 1) + k) * q_count + j
        pltpu.make_async_copy(gbuf.at[slot], gbuf.at[slot], grecv.at[sem]).wait()

    def conv(j, _):
        lanes = pl.ds(pl.multiple_of(j * LANES, LANES), LANES)
        taps = fbuf[:, lanes]
        high = taps.astype(BF16)
        low = (taps - high.astype(F32)).astype(BF16)
        spec = mm2(fil_ref[...], high) + mm(fil_ref[: 3 * BLOCK], low)
        a, b, c = spec[:BLOCK], spec[BLOCK : 2 * BLOCK], spec[2 * BLOCK :]
        for block in range(blocks - 1, -1, -1):
            if block == 0:
                window = jnp.concatenate([halo[:, lanes], kbuf[:BLOCK, lanes]], 0)
            else:
                window = kbuf[(block - 1) * BLOCK : (block + 1) * BLOCK, lanes]
            x = mm2(fwd_ref[...], window)
            xr, xi = x[:BLOCK], x[BLOCK:]
            y = jnp.concatenate([xr * a - xi * b, xr * b + xi * c], 0).astype(BF16)
            filtered = mm2(back_ref[...], y)
            r = slice(block * BLOCK, (block + 1) * BLOCK)
            gbuf[z * q_count + j, r] = (qbuf[r, lanes].astype(F32) * filtered).astype(BF16)

        @pl.when(z < m - 1)
        def _():
            g_copy(True, 0, j).start()

        @pl.when(z > 0)
        def _():
            g_copy(False, 0, j).start()

        return 0

    lax.fori_loop(0, q_count, conv, 0)
    halo_copy.wait_send()
    load_kl = local(6, kli_hbm, kbuf)
    load_kl.start()
    load_ql = local(7, qli_hbm, qbuf)
    load_ql.start()

    steps = [(k, j) for k in range(m - 1) for j in range(q_count)]
    done = 0
    for i, (k, j) in enumerate(steps):

        @pl.when(z - 1 - k >= 0)
        def _():
            g_recv(True, k, j)

            if k < m - 2:

                @pl.when(z < m - 1)
                def _():
                    g_copy(True, k + 1, j).start()

        @pl.when(z + 1 + k < m)
        def _():
            g_recv(False, k, j)

            if k < m - 2:

                @pl.when(z > 0)
                def _():
                    g_copy(False, k + 1, j).start()

        until = len(events) * (i + 1) // len(steps)
        for d, p, hops in events[done:until]:
            wait_w(d, p)
            for hop in hops:
                send_w(d, p, hop)
        done = until
    for d, p in tail:
        wait_w(d, p)
    load_w.wait()

    def multiply(step, _):
        g = step // (chans // LANES)
        cols = pl.ds(pl.multiple_of(lax.rem(step, chans // LANES) * LANES, LANES), LANES)
        part = mm(gbuf[g], wbuf[pl.ds(pl.multiple_of(g * LANES, LANES), LANES), cols])

        @pl.when(g == 0)
        def _():
            acc[:, cols] = part

        @pl.when(g > 0)
        def _():
            acc[:, cols] += part

        return 0

    lax.fori_loop(0, (m * q_count) * (chans // LANES), multiply, 0)
    load_r.wait()
    load_kl.wait()
    load_ql.wait()

    row = lax.broadcasted_iota(jnp.int32, (8, LANES), 0)

    def scan_lanes(j, _):
        lanes = pl.ds(pl.multiple_of(j * LANES, LANES), LANES)
        rate = jnp.broadcast_to(rate_ref[:, lanes], (8, LANES))
        power = jnp.exp(-rate * (row + 1).astype(F32))
        masked = [jnp.where(row >= s, jnp.exp(-rate * float(s)), 0.0) for s in (1, 2, 4)]

        def tile(t, last):
            r = pl.ds(pl.multiple_of(t * 16, 16), 16)
            value = (vbuf[r, lanes].astype(F32) + acc[r, lanes]).astype(BF16)
            vbuf[r, lanes] = value
            drive = kbuf[r, lanes].astype(F32) * value.astype(F32)
            out = []
            for h in range(2):
                x = drive[8 * h : 8 * h + 8]
                for s, coef in zip((1, 2, 4), masked):
                    x = x + coef * pltpu.roll(x, s, 0)
                x = x + power * last
                last = jnp.broadcast_to(x[7:8], (8, LANES))
                out.append(x)
            acc[r, lanes] = jnp.concatenate(out, 0)
            return last

        lax.fori_loop(0, rows // 16, tile, jnp.zeros((8, LANES), F32))
        return 0

    lax.fori_loop(0, chans // LANES, scan_lanes, 0)
    store_mixed = local(8, vbuf, mixed_hbm)
    store_mixed.start()

    def end_copy(d):
        return pltpu.make_async_remote_copy(
            src_ref=acc.at[pl.ds(rows - 8, 8)],
            dst_ref=ends.at[d],
            send_sem=esend.at[d],
            recv_sem=erecv.at[d],
            device_id={"ctx": lax.rem(me + d, n)},
            device_id_type=MESH,
        )

    for d in range(1, n):

        @pl.when(me + d < n)
        def _():
            end_copy(d).start()

    carry[...] = jnp.zeros_like(carry)
    jump = jnp.exp(-rate_ref[...] * float(rows))
    for d in range(n - 1, 0, -1):

        @pl.when(me >= d)
        def _():
            pltpu.make_async_copy(ends.at[d], ends.at[d], erecv.at[d]).wait()
            carry[...] = carry[...] * jump + ends[d, 7:8]

    def finish_lanes(j, _):
        lanes = pl.ds(pl.multiple_of(j * LANES, LANES), LANES)
        rate = jnp.broadcast_to(rate_ref[:, lanes], (8, LANES))
        scale = scale_ref[:, lanes]
        jump8 = jnp.exp(-rate * 8.0)
        first = carry[:, lanes] * jnp.exp(-rate * (row + 1).astype(F32))

        def tile(t, add):
            r = pl.ds(pl.multiple_of(t * 16, 16), 16)
            later = add * jump8
            state = acc[r, lanes] + jnp.concatenate([add, later], 0)
            qbuf[r, lanes] = (qbuf[r, lanes].astype(F32) * scale * state).astype(BF16)
            return later * jump8

        lax.fori_loop(0, rows // 16, tile, first)
        return 0

    lax.fori_loop(0, chans // LANES, finish_lanes, 0)
    store_long = local(9, qbuf, long_hbm)
    store_long.start()
    for copy in sends:
        copy.wait_send()
    for k, j in steps:

        @pl.when(jnp.logical_and(z - k >= 0, z < m - 1))
        def _():
            g_copy(True, k, j).wait_send()

        @pl.when(jnp.logical_and(z + k < m, z > 0))
        def _():
            g_copy(False, k, j).wait_send()

    for d in range(1, n):

        @pl.when(me + d < n)
        def _():
            end_copy(d).wait_send()

    store_mixed.wait()
    store_long.wait()


def body(n, m, resid_in, q_mr, k_mr, v_mr, mr_filter, mr_out, q_li, k_li, li_rate, li_residue):
    rows, chans = q_mr.shape
    taps = mr_filter.shape[0]
    assert taps == BLOCK
    pieces = mr_out.shape[0] // PIECE
    depth = mr_out.shape[0] * n
    q_count = chans // LANES
    forward, of_filter, back = (jnp.asarray(t) for t in transforms())
    own, events, _ = w_plan(n, pieces)
    send_count = len(own) + sum(len(hops) for _, _, hops in events)
    scale = li_residue * jnp.sqrt(-jnp.expm1(-2.0 * li_rate))
    hbm = pl.BlockSpec(memory_space=pl.ANY)
    vmem = pl.BlockSpec(memory_space=pltpu.VMEM)
    out = jax.ShapeDtypeStruct((rows, chans), BF16)
    dma = pltpu.SemaphoreType.DMA
    streams = 2 * (m - 1) * q_count
    return pl.pallas_call(
        functools.partial(kernel, n, m, pieces),
        out_shape=(out, out),
        in_specs=[hbm] * 8 + [vmem] * 5,
        out_specs=(hbm, hbm),
        scratch_shapes=[
            pltpu.VMEM((rows, chans), BF16),
            pltpu.VMEM((rows, chans), BF16),
            pltpu.VMEM((rows, chans), BF16),
            pltpu.VMEM((taps, chans), F32),
            pltpu.VMEM((BLOCK, chans), BF16),
            pltpu.VMEM((depth, chans), BF16),
            pltpu.VMEM((m * q_count, rows, LANES), BF16),
            pltpu.VMEM((rows, chans), F32),
            pltpu.VMEM((n, 8, chans), F32),
            pltpu.VMEM((8, chans), F32),
            dma((10,)),
            dma((send_count,)),
            dma((n * pieces,)),
            dma((streams,)),
            dma((streams,)),
            dma((2,)),
            dma((n,)),
            dma((n,)),
        ],
        compiler_params=pltpu.CompilerParams(
            collective_id=0, has_side_effects=True, vmem_limit_bytes=60 * 1024 * 1024
        ),
    )(
        resid_in, q_mr, k_mr, v_mr, mr_filter, mr_out, q_li, k_li,
        li_rate[None, :], scale[None, :], forward, of_filter, back,
    )


def solution(mesh):
    both = P("ctx", "mp")
    in_specs = (both, both, both, both, P(None, "mp"), both, both, both, P("mp"), P("mp"))
    fn = functools.partial(body, mesh.shape["ctx"], mesh.shape["mp"])
    return jax.shard_map(fn, mesh=mesh, in_specs=in_specs, out_specs=(both, both), check_vma=False)
```

time: 566 us -> 272 us (0.48)
  waiting for transfers between devices: 300 us -> 0 us
  Pallas kernels: 0 us -> 262 us
  local copies, waits for them, and re-layouts: 111 us -> 4.63 us
  matrix products: 71.2 us -> 0 us
  other arithmetic: 40.3 us -> 1.34 us
  blocking collectives: 23.3 us -> 0 us
  between operations: 14.7 us -> 0.65 us
    all_gather x2 -> x0, waiting for transfers between devices: 299 us -> none  [the longest x1 161 us: body(): all_rows = lax.all_gather(mr_out, 'ctx', axis=0, tiled=True)]
    pallas_call x0 -> x1, Pallas kernels: none -> 262 us  [body(): pl.pallas_call(functools.partial(kernel, n, m, pieces), out_shape=(out, o...]
    slice x35 -> x0, local copies, waits for them, and re-layouts: 62.4 us -> none  [the longest x34 61.5 us: body(): lax.associative_scan(link_pair, (decay_rows, drive_li), axis=0)]
    conv_general_dilated x1 -> x0, matrix products: 45.6 us -> none  [body(): lax.conv_general_dilated(padded, kernel, (1,), 'VALID', dimension_numbers...]
    pad x16 -> x0, local copies, waits for them, and re-layouts: 35.5 us -> none  [body(): lax.associative_scan(link_pair, (decay_rows, drive_li), axis=0)]
    dot_general x1 -> x0, matrix products: 25.6 us -> none  [body(): summed = jnp.dot(gathered, all_rows, preferred_element_type=jnp.float32)]
    all_gather x2 -> x0, blocking collectives: 23.3 us -> none  [carried_in(): pieces = jax.tree.map(lambda part: lax.all_gather(part, axis), value)]
    add x25 -> x0, other arithmetic: 21.4 us -> none  [the longest x16 16.2 us: link_pair(): return (earlier[0] * later[0], later[0] * earlier[1] + later[1])]
  transfers between devices with their start and end apart: 3 -> 0, of which waited for: 2 -> 0; matrix products, arithmetic and copies ran while one was open for 1% -> 0% of each run, Pallas kernels for 0% -> 0%
where the time goes in v1:
time: 272 us; the launch traced here: 268 us
  Pallas kernels  262 us (96%)
  local copies, waits for them, and re-layouts  4.63 us (2%)
    pallas_call x1, Pallas kernels, body(): pl.pallas_call(functools.partial(kernel, n, m, pieces), out_shape=(out, o...  262 us

profile of v1, /device:TPU:0, one launch (start us, length us, event | category | flops | bytes accessed | tf_op | source)
XLA Modules:
  0.0 268.2 jit_solution(4258838077817629655)
XLA Ops:
  0.6 1.3 sqrt_multiply_fusion
  2.0 261.6 %shard_map.140 = (bf16[512,2048]{1,0:T(8,128)(2,1)}, bf16[512,2048]{1,0:T(8,128)(2,1)}) custom-call(bf16[512,2048]{1,0:T(8,128)(2,1)} %resid_hbm.1, bf16[512,2048]{1,0:T(8,128)(2,1)} %q_hbm.1, bf16[512,2048]{1,0:T(8,128)(2,1)} %k_hbm.1, bf16[512,2048]{1,0:T(8,128)(2,1)} %v_hbm.1, f32[128,2048]{1,0:T(8,128)} %filt_hbm.1, bf16[1024,2048]{1,0:T(8,128)(2,1)} %w_hbm.1, ...), custom_call_target="tpu_custom_call" | custom-call | tf_op jit(solution)/shard_map/pallas_call | solution.py:403
  263.6 0.0 copy-start
  263.6 3.3 %copy.17 = bf16[512,2048]{1,0:T(8,128)(2,1)} copy(bf16[512,2048]{1,0:T(8,128)(2,1)} %get-tuple-element.4) | data formatting | bytes 4194304
  266.9 0.0 copy-done
  266.9 1.3 copy.18
Async XLA Ops:
  263.6 3.3 %copy-start = (bf16[512,2048]{1,0:T(8,128)(2,1)S(1)}, bf16[512,2048]{1,0:T(8,128)(2,1)}, u32[]{:S(2)}) copy-start(bf16[512,2048]{1,0:T(8,128)(2,1)} %get-tuple-element.5) | copy-start | bytes 6291460

commit v2 on v1

--- a/solution.py
+++ b/solution.py
@@ -13,6 +13,7 @@
 PIECE = 256
 LANES = 512
 BLOCK = 128
+ORDER = [0, 0, 0, 0, 0, 0, 0, 8, 12, 12, 12, 12]
 MESH = pl.DeviceIdType.MESH
 
 
@@ -232,6 +233,24 @@
     load_ql = local(7, qli_hbm, qbuf)
     load_ql.start()
 
+    def multiply_zone(zone):
+        def multiply(step, _):
+            cols = pl.ds(pl.multiple_of(step * LANES, LANES), LANES)
+            total = acc[:, cols]
+            for g in range(zone * q_count, (zone + 1) * q_count):
+                total = total + mm(gbuf[g], wbuf[g * LANES : (g + 1) * LANES, cols])
+            acc[:, cols] = total
+            return 0
+
+        lax.fori_loop(0, chans // LANES, multiply, 0)
+
+    early = n == 8 and m == 4 and bool(events)
+
+    def ready_early(zone):
+        near = jnp.logical_and(zone >= z - 1, zone <= z + 1)
+        return jnp.logical_and(near, me // 2 != 3 - zone)
+
+    acc[...] = jnp.zeros_like(acc)
     steps = [(k, j) for k in range(m - 1) for j in range(q_count)]
     done = 0
     for i, (k, j) in enumerate(steps):
@@ -256,32 +275,30 @@
                 def _():
                     g_copy(False, k + 1, j).start()
 
-        until = len(events) * (i + 1) // len(steps)
+        until = ORDER[i] if early and len(steps) == 12 else len(events)
         for d, p, hops in events[done:until]:
             wait_w(d, p)
             for hop in hops:
                 send_w(d, p, hop)
         done = until
+        if early and i == 2 * q_count - 1:
+            for d, p in tail:
+                if d != 7:
+                    wait_w(d, p)
+            load_w.wait()
+            for zone in range(m):
+                pl.when(ready_early(zone))(functools.partial(multiply_zone, zone))
     for d, p in tail:
-        wait_w(d, p)
-    load_w.wait()
-
-    def multiply(step, _):
-        g = step // (chans // LANES)
-        cols = pl.ds(pl.multiple_of(lax.rem(step, chans // LANES) * LANES, LANES), LANES)
-        part = mm(gbuf[g], wbuf[pl.ds(pl.multiple_of(g * LANES, LANES), LANES), cols])
-
-        @pl.when(g == 0)
-        def _():
-            acc[:, cols] = part
-
-        @pl.when(g > 0)
-        def _():
-            acc[:, cols] += part
-
-        return 0
-
-    lax.fori_loop(0, (m * q_count) * (chans // LANES), multiply, 0)
+        if d == 7 or not early:
+            wait_w(d, p)
+    if not early:
+        load_w.wait()
+    for zone in range(m):
+        if early:
+            pl.when(jnp.logical_not(ready_early(zone)))(functools.partial(multiply_zone, zone))
+        else:
+            multiply_zone(zone)
+
     load_r.wait()
     load_kl.wait()
     load_ql.wait()

time: 272 us -> 254 us (0.934)
  Pallas kernels: 262 us -> 244 us
    pallas_call x1, Pallas kernels: 262 us -> 244 us  [body(): pl.pallas_call(functools.partial(kernel, n, m, pieces), out_shape=(out, o...]
where the time goes in v2:
time: 254 us; the launch traced here: 250 us
  Pallas kernels  244 us (96%)
  local copies, waits for them, and re-layouts  4.63 us (2%)
    pallas_call x1, Pallas kernels, body(): pl.pallas_call(functools.partial(kernel, n, m, pieces), out_shape=(out, o...  244 us

profile of v2, /device:TPU:0, one launch (start us, length us, event | category | flops | bytes accessed | tf_op | source)
XLA Modules:
  0.0 250.5 jit_solution(5524019672180403667)
XLA Ops:
  0.6 1.3 sqrt_multiply_fusion
  2.0 243.9 %shard_map.140 = (bf16[512,2048]{1,0:T(8,128)(2,1)}, bf16[512,2048]{1,0:T(8,128)(2,1)}) custom-call(bf16[512,2048]{1,0:T(8,128)(2,1)} %resid_hbm.1, bf16[512,2048]{1,0:T(8,128)(2,1)} %q_hbm.1, bf16[512,2048]{1,0:T(8,128)(2,1)} %k_hbm.1, bf16[512,2048]{1,0:T(8,128)(2,1)} %v_hbm.1, f32[128,2048]{1,0:T(8,128)} %filt_hbm.1, bf16[1024,2048]{1,0:T(8,128)(2,1)} %w_hbm.1, ...), custom_call_target="tpu_custom_call" | custom-call | tf_op jit(solution)/shard_map/pallas_call | solution.py:420
  245.8 0.0 copy-start
  245.8 3.3 %copy.17 = bf16[512,2048]{1,0:T(8,128)(2,1)} copy(bf16[512,2048]{1,0:T(8,128)(2,1)} %get-tuple-element.4) | data formatting | bytes 4194304
  249.2 0.0 copy-done
  249.2 1.3 copy.18
Async XLA Ops:
  245.8 3.3 %copy-start = (bf16[512,2048]{1,0:T(8,128)(2,1)S(1)}, bf16[512,2048]{1,0:T(8,128)(2,1)}, u32[]{:S(2)}) copy-start(bf16[512,2048]{1,0:T(8,128)(2,1)} %get-tuple-element.5) | copy-start | bytes 6291460
